TPU v7x, 32 devices: a whole 2x2x4 slice. The times are simulated.
32 devices in a mesh: cube: 4 (over y, x), panel: 8 (over z, core).
Axes of the slice: x: 2, y: 2, z: 4, core: 2. Of those that a mesh axis runs over, the one named last changes fastest.
Arguments:
- columns: bfloat16 [96, 4, 4096], P('cube', None, 'panel'), may hold values from -8 to 8
- leaf_of: int32 [96, 1], P('cube'), may hold values from 0 to 3; in each aligned block of 24 rows (0 to 23, 24 to 47, ...) at most 12 rows name the same one
- inverse_root: bfloat16 [4096, 4096], P('cube', 'panel'), may hold values from -0.5 to 0.5, as said below
- inverse_upper: bfloat16 [8192, 4096], P('cube', 'panel'), may hold values from -0.5 to 0.5, as said below
- inverse_middle: bfloat16 [16384, 4096], P('cube', 'panel'), may hold values from -0.5 to 0.5, as said below
- inverse_leaf: bfloat16 [16384, 4096], P('cube', 'panel'), may hold values from -0.5 to 0.5, as said below
- coupling_upper: bfloat16 [8192, 1, 4096], P('cube', None, 'panel'), may hold values from -6 to 6
- coupling_middle: bfloat16 [16384, 2, 4096], P('cube', None, 'panel'), may hold values from -6 to 6
- coupling_leaf: bfloat16 [16384, 3, 4096], P('cube', None, 'panel'), may hold values from -6 to 6
Outputs:
- core_factor: float32 [192, 192], replicated
- project_root: bfloat16 [4096, 192], P(('cube', 'panel'))
- project_upper: bfloat16 [8192, 96], P(('cube', 'panel'))
- project_middle: bfloat16 [16384, 48], P(('cube', 'panel'))
- project_leaf: bfloat16 [16384, 48], P(('cube', 'panel'))
Inputs may be any that keep to these rules, and one draw needn't show every extreme that they name: `leaf_of`: among the 24 columns held by one index of cube, no leaf is named more than 12 times. `inverse_root`: each block of 4096 rows is lower triangular. `inverse_upper`: each block of 4096 rows is lower triangular. `inverse_middle`: each block of 4096 rows is lower triangular. `inverse_leaf`: each block of 4096 rows is lower triangular.
All inputs are finite; a program needn't handle non-finite values.
Results may differ from a plain program's by a relative error of at most 0.011.
Values may be sent and summed in bfloat16 or wider, within the bound.
A program may use at most 128 MiB of HBM per device.

v0:
```python
import jax
import jax.numpy as jnp
from jax import lax
from jax.sharding import PartitionSpec as P


def from_partner(value, axis, bit):
    mask = 2**bit
    pairs = [(source, source ^ mask) for source in range(lax.axis_size(axis))]
    return lax.ppermute(value, axis, pairs)


def pair_concat(block_cols, group_bits, cube_index):
    for bit_pos in range(group_bits):
        partner = from_partner(block_cols, "cube", bit_pos)
        keeps_low = cube_index >> bit_pos & 1 == 0
        block_cols = jnp.where(
            keeps_low,
            jnp.concatenate([block_cols, partner], 0),
            jnp.concatenate([partner, block_cols], 0),
        )
    return block_cols


def pair_total(joined, group_bits):
    for bit_pos in range(group_bits):
        partner = from_partner(joined.astype(jnp.bfloat16), "cube", bit_pos).astype(joined.dtype)
        joined = joined + partner
    return joined


def body(
    columns,
    leaf_of,
    inverse_root,
    inverse_upper,
    inverse_middle,
    inverse_leaf,
    coupling_upper,
    coupling_middle,
    coupling_leaf,
):
    cube_size = lax.axis_size("cube")
    panel_size = lax.axis_size("panel")
    cube_index = lax.axis_index("cube")
    panel_index = lax.axis_index("panel")
    time_cols = columns.shape[0]
    stripe = columns.shape[2]
    leaves = min(8, cube_size)
    leaf_share = cube_size // leaves
    capacity = leaf_share * max(1, (2 * time_cols // leaves + leaf_share - 1) // leaf_share)
    per_slot = capacity // leaf_share
    dev_cols = cube_size * per_slot
    labels = leaf_of[:, 0]
    onehot = (labels[:, None] == jnp.arange(leaves, dtype=jnp.int32)[None, :]).astype(jnp.int32)
    before = jnp.cumsum(onehot, axis=0, dtype=jnp.int32) - onehot
    within = jnp.sum(before * onehot, axis=1, dtype=jnp.int32)
    target = labels * capacity + within
    dispatch = (target[None, :] == jnp.arange(leaves * capacity, dtype=jnp.int32)[:, None]).astype(
        jnp.bfloat16
    )
    packed = jnp.dot(
        dispatch, columns.reshape(time_cols, 4 * stripe), preferred_element_type=jnp.float32
    ).astype(jnp.bfloat16)
    packed = packed.reshape(cube_size, per_slot, 4, stripe)
    arrived = lax.all_to_all(packed, "cube", split_axis=0, concat_axis=0, tiled=True)
    front_cols = arrived.reshape(dev_cols, 4, stripe)
    inverses = (inverse_root, inverse_upper, inverse_middle, inverse_leaf)
    couplings = (None, coupling_upper, coupling_middle, coupling_leaf)
    outputs = [None, None, None, None]
    factor = None
    for tree_level in (3, 2, 1, 0):
        node_count = min(2**tree_level, cube_size)
        group_size = cube_size // node_count
        group_bits = group_size.bit_length() - 1
        group_width = group_size * dev_cols
        group_rank = cube_index % group_size
        if group_size > 1:
            group_cols = pair_concat(front_cols, group_bits, cube_index)
        else:
            group_cols = front_cols
        inverse = inverses[tree_level]
        local_rows = inverse.shape[0]
        panel_rows = local_rows // panel_size
        top_rows = group_cols[:, 0, :]
        term_full = lax.dot_general(
            inverse, top_rows, (((1,), (1,)), ((), ())), preferred_element_type=jnp.float32
        )
        projected = lax.psum(term_full, "panel").astype(jnp.bfloat16)
        own_part = lax.dynamic_slice_in_dim(projected, panel_index * panel_rows, panel_rows, 0)
        gram_part = lax.dot_general(
            projected, projected, (((0,), (0,)), ((), ())), preferred_element_type=jnp.float32
        )
        outputs[tree_level] = own_part
        if tree_level > 0:
            coupling = couplings[tree_level].reshape(local_rows, tree_level * stripe)
            cross_term = lax.dot_general(
                projected, coupling, (((0,), (0,)), ((), ())), preferred_element_type=jnp.float32
            )
            rest_cols = (
                group_cols[:, 1:, :].reshape(group_width, tree_level * stripe).astype(jnp.float32)
            )
            summed_all = pair_total(jnp.concatenate([gram_part, cross_term], 1), group_bits)
            gram_total = summed_all[:, :group_width]
            factor = jnp.linalg.cholesky(jnp.eye(group_width, dtype=jnp.float32) + gram_total)
            remainder = rest_cols - summed_all[:, group_width:]
            solved = jax.scipy.linalg.solve_triangular(factor, remainder, lower=True).astype(
                jnp.bfloat16
            )
            own_solved = lax.dynamic_slice_in_dim(solved, group_rank * dev_cols, dev_cols, 0)
            front_cols = own_solved.reshape(dev_cols, tree_level, stripe)
        else:
            gram_total = pair_total(gram_part, group_bits)
            factor = jnp.linalg.cholesky(jnp.eye(group_width, dtype=jnp.float32) + gram_total)
    return (factor, outputs[0], outputs[1], outputs[2], outputs[3])


def solution(mesh):
    in_specs = (
        P("cube", None, "panel"),
        P("cube", None),
        P("cube", "panel"),
        P("cube", "panel"),
        P("cube", "panel"),
        P("cube", "panel"),
        P("cube", None, "panel"),
        P("cube", None, "panel"),
        P("cube", None, "panel"),
    )
    out_specs = (
        P(),
        P(("cube", "panel"), None),
        P(("cube", "panel"), None),
        P(("cube", "panel"), None),
        P(("cube", "panel"), None),
    )
    return jax.shard_map(body, mesh=mesh, in_specs=in_specs, out_specs=out_specs, check_vma=False)
```

profile of v0, /device:TPU:0, one launch (start us, length us, event | category | flops | bytes accessed | tf_op | source)
XLA Modules:
  0.0 306.9 jit_solution(17669139950447691569)
XLA Ops:
  5.0 5.2 %all-to-all-start = ((bf16[4,12,4,512]{3,2,1,0:T(4,128)(2,1)}), bf16[4,12,4,512]{3,2,1,0:T(4,128)(2,1)S(1)}, u32[]{:S(2)}, u32[]{:S(2)}) async-start(bf16[4,12,4,512]{3,2,1,0:T(4,128)(2,1)} %reshape.183), calls=%async_computation | async-start | bytes 393216 | tf_op jit(solution)/shard_map/all_to_all | solution.py:66
  10.2 16.9 %copy.38 = bf16[4096,3,512]{0,2,1:T(8,128)(2,1)} copy(bf16[4096,3,512]{2,0,1:T(8,128)(2,1)} %param.18) | data formatting | bytes 25165824 | tf_op args[8]
  27.1 9.3 %copy.57 = bf16[512,8,2,512]{3,1,2,0:T(8,128)(2,1)} copy(bf16[512,8,2,512]{3,2,1,0:T(2,128)(2,1)} %bitcast.108) | data formatting | bytes 16777216
  36.6 4.4 %convolution_bitcast_fusion.1 = f32[4096,48]{0,1:T(8,128)} fusion(bf16[4096,512]{1,0:T(8,128)(2,1)} %param.15, bf16[48,1,512]{2,1,0:T(2,128)(2,1)S(1)} %slice.92), kind=kOutput, calls=%fused_computation.1 | convolution fusion | flops 201326592 | bytes 5029888 | tf_op jit(solution)/shard_map/dot_general | solution.py:86
  41.0 37.0 %all-reduce.5 = bf16[4096,48]{0,1:T(8,128)(2,1)S(1)} all-reduce(f32[4096,48]{0,1:T(8,128)} %convolution_bitcast_fusion.1), channel_id=1, replica_groups=mesh['cube'=4,'panel'=8] {'panel'}, use_global_device_ids=true, to_apply=%region_2.3 | all-reduce | flops 196608 | bytes 1179648 | tf_op jit(solution)/shard_map/psum | solution.py:89
  78.4 4.4 %cholesky.205 = f32[48,48]{1,0:T(8,128)S(1)} custom-call(f32[48,48]{1,0:T(8,128)S(1)} %fusion.28), custom_call_target="Cholesky" | custom-call | tf_op jit(solution)/shard_map/jit(cholesky)/cholesky | solution.py:105
  84.1 3.7 %custom-call.28 = f32[1,48,48]{1,2,0:T(8,128)S(1)} custom-call(f32[1,48,48]{2,1,0:T(8,128)S(1)} %fusion.23), custom_call_target="InvertDiagBlocksLowerTriangular" | custom-call | tf_op jit(solution)/shard_map/jit(_solve_triangular)/triangular_solve | solution.py:107
  87.8 8.5 %convolution_subtract_fusion = f32[48,1536]{1,0:T(8,128)S(1)} fusion(f32[48,1536]{1,0:T(8,128)S(1)} %bitcast.112, bf16[4096,48]{0,1:T(8,128)(2,1)S(1)} %all-reduce.5, bf16[4096,1536]{0,1:T(8,128)(2,1)} %bitcast.107), kind=kOutput, calls=%fused_computation.3 | convolution fusion | flops 604053504 | bytes 13565952 | tf_op jit(solution)/shard_map/dot_general | solution.py:97
  97.0 4.4 %convolution_bitcast_fusion = f32[4096,48]{0,1:T(8,128)} fusion(bf16[4096,512]{1,0:T(8,128)(2,1)} %param.14, bf16[48,1,512]{2,1,0:T(2,128)(2,1)S(1)} %slice.94), kind=kOutput, calls=%fused_computation | convolution fusion | flops 201326592 | bytes 5029888 | tf_op jit(solution)/shard_map/dot_general | solution.py:86
  101.5 34.9 %all-reduce.6 = bf16[4096,48]{0,1:T(8,128)(2,1)S(1)} all-reduce(f32[4096,48]{0,1:T(8,128)} %convolution_bitcast_fusion), channel_id=1, replica_groups=mesh['cube'=4,'panel'=8] {'panel'}, use_global_device_ids=true, to_apply=%region_5.7 | all-reduce | flops 196608 | bytes 1179648 | tf_op jit(solution)/shard_map/psum | solution.py:89
  136.7 4.4 %cholesky.216 = f32[48,48]{1,0:T(8,128)S(1)} custom-call(f32[48,48]{1,0:T(8,128)S(1)} %fusion.26), custom_call_target="Cholesky" | custom-call | tf_op jit(solution)/shard_map/jit(cholesky)/cholesky | solution.py:105
  142.4 3.7 %custom-call.29 = f32[1,48,48]{1,2,0:T(8,128)S(1)} custom-call(f32[1,48,48]{2,1,0:T(8,128)S(1)} %fusion.24), custom_call_target="InvertDiagBlocksLowerTriangular" | custom-call | tf_op jit(solution)/shard_map/jit(_solve_triangular)/triangular_solve | solution.py:107
  146.1 5.0 %convolution_subtract_fusion.1 = f32[48,1024]{1,0:T(8,128)S(1)} fusion(f32[48,1024]{1,0:T(8,128)S(1)} %bitcast.113, bf16[4096,48]{0,1:T(8,128)(2,1)S(1)} %all-reduce.6, bf16[4096,1024]{1,0:T(8,128)(2,1)} %bitcast.106), kind=kOutput, calls=%fused_computation.9 | convolution fusion | flops 402702336 | bytes 9175040 | tf_op jit(solution)/shard_map/dot_general | solution.py:97
  158.0 35.8 %all-reduce.7 = bf16[2048,96]{0,1:T(8,128)(2,1)S(1)} all-reduce(f32[2048,96]{0,1:T(8,128)} %convolution_bitcast_fusion.2), channel_id=1, replica_groups=mesh['cube'=4,'panel'=8] {'panel'}, use_global_device_ids=true, to_apply=%region_6.8 | all-reduce | flops 196608 | bytes 1179648 | tf_op jit(solution)/shard_map/psum | solution.py:89
  201.4 8.8 %cholesky.92 = f32[96,96]{1,0:T(8,128)S(1)} custom-call(f32[96,96]{1,0:T(8,128)S(1)} %fusion.21), custom_call_target="Cholesky" | custom-call | tf_op jit(solution)/shard_map/jit(cholesky)/cholesky | solution.py:105
  211.6 7.4 %custom-call.30 = f32[1,96,96]{1,2,0:T(8,128)S(1)} custom-call(f32[1,96,96]{2,1,0:T(8,128)S(1)} %fusion.15), custom_call_target="InvertDiagBlocksLowerTriangular" | custom-call | tf_op jit(solution)/shard_map/jit(_solve_triangular)/triangular_solve | solution.py:107
  220.4 3.1 %collective-permute-done.2 = bf16[48,1,512]{2,0,1:T(8,128)(2,1)S(1)} collective-permute-done((bf16[48,1,512]{2,0,1:T(8,128)(2,1)S(1)}, bf16[48,1,512]{2,0,1:T(8,128)(2,1)S(1)}, u32[]{:S(2)}, u32[]{:S(2)}) %collective-permute-start.2) | collective-permute-done | bytes 49184 | tf_op jit(solution)/shard_map/ppermute | solution.py:10
  224.7 3.6 %collective-permute-done.3 = bf16[96,1,512]{2,0,1:T(8,128)(2,1)S(1)} collective-permute-done((bf16[96,1,512]{2,0,1:T(8,128)(2,1)S(1)}, bf16[96,1,512]{2,0,1:T(8,128)(2,1)S(1)}, u32[]{:S(2)}, u32[]{:S(2)}) %collective-permute-start.3) | collective-permute-done | bytes 98336 | tf_op jit(solution)/shard_map/ppermute | solution.py:10
  230.8 34.9 %all-reduce.8 = bf16[1024,192]{0,1:T(8,128)(2,1)S(1)} all-reduce(f32[1024,192]{0,1:T(8,128)} %convolution_bitcast_fusion.3), channel_id=1, replica_groups=mesh['cube'=4,'panel'=8] {'panel'}, use_global_device_ids=true, to_apply=%region_9.11 | all-reduce | flops 196608 | bytes 1179648 | tf_op jit(solution)/shard_map/psum | solution.py:89
  267.7 3.0 collective-permute-done.4
  272.5 2.9 collective-permute-done.5
  275.7 11.7 %cholesky.154 = f32[128,128]{1,0:T(8,128)S(1)} custom-call(f32[128,128]{1,0:T(8,128)S(1)} %cholesky.225), custom_call_target="Cholesky" | custom-call | tf_op jit(solution)/shard_map/jit(cholesky)/cholesky | solution.py:114
  287.5 9.8 %custom-call.31 = f32[1,128,128]{1,2,0:T(8,128)S(1)} custom-call(f32[1,128,128]{2,1,0:T(8,128)S(1)} %get-tuple-element.7), custom_call_target="InvertDiagBlocksLowerTriangular" | custom-call | tf_op jit(solution)/shard_map/jit(cholesky)/cholesky | solution.py:114
  297.7 5.8 %cholesky.174 = f32[64,64]{1,0:T(8,128)S(1)} custom-call(f32[64,64]{1,0:T(8,128)S(1)} %convolution_subtract_fusion.2), custom_call_target="Cholesky" | custom-call | tf_op jit(solution)/shard_map/jit(cholesky)/cholesky | solution.py:114
  (76 shorter events, 36.2 us)
Async XLA Ops:
  0.6 155.7 %copy-start = (bf16[2048,512]{1,0:T(8,128)(2,1)S(1)}, bf16[2048,512]{1,0:T(8,128)(2,1)}, u32[]{:S(2)}) copy-start(bf16[2048,512]{1,0:T(8,128)(2,1)} %param.13) | copy-start | bytes 6291460
  5.0 31.4 %all-to-all-start = ((bf16[4,12,4,512]{3,2,1,0:T(4,128)(2,1)}), bf16[4,12,4,512]{3,2,1,0:T(4,128)(2,1)S(1)}, u32[]{:S(2)}, u32[]{:S(2)}) async-start(bf16[4,12,4,512]{3,2,1,0:T(4,128)(2,1)} %reshape.183), calls=%async_computation | async-start | bytes 393216 | tf_op jit(solution)/shard_map/all_to_all | solution.py:66
  151.4 4.9 %collective-permute-start = (bf16[48,2,512]{2,0,1:T(8,128)(2,1)S(1)}, bf16[48,2,512]{2,0,1:T(8,128)(2,1)S(1)}, u32[]{:S(2)}, u32[]{:S(2)}) collective-permute-start(bf16[48,2,512]{2,0,1:T(8,128)(2,1)S(1)} %bitcast.115), channel_id=1, source_target_pairs={{0,8},{8,0},{16,24},{24,16},{1,9},{9,1},{17,25},{25,17},{2,10},{10... | collective-permute-start | bytes 294920 | tf_op jit(solution)/shard_map/ppermute | solution.py:10
  196.2 4.9 %collective-permute-start.1 = (bf16[96,608]{1,0:T(8,128)(2,1)S(1)}, bf16[96,608]{1,0:T(8,128)(2,1)S(1)}, u32[]{:S(2)}, u32[]{:S(2)}) collective-permute-start(bf16[96,608]{1,0:T(8,128)(2,1)S(1)} %fusion.2), channel_id=1, source_target_pairs={{0,8},{8,0},{16,24},{24,16},{1,9},{9,1},{17,25},{25,17},{2,10},{10... | collective-permute-start | bytes 350216 | tf_op jit(solution)/shard_map/ppermute | solution.py:10
  219.4 4.2 %collective-permute-start.2 = (bf16[48,1,512]{2,0,1:T(8,128)(2,1)S(1)}, bf16[48,1,512]{2,0,1:T(8,128)(2,1)S(1)}, u32[]{:S(2)}, u32[]{:S(2)}) collective-permute-start(bf16[48,1,512]{2,0,1:T(8,128)(2,1)S(1)} %fusion.58), channel_id=1, source_target_pairs={{0,8},{8,0},{16,24},{24,16},{1,9},{9,1},{17,25},{25,17},{2,10},{10... | collective-permute-start | bytes 147464 | tf_op jit(solution)/shard_map/ppermute | solution.py:10
  223.6 4.7 %collective-permute-start.3 = (bf16[96,1,512]{2,0,1:T(8,128)(2,1)S(1)}, bf16[96,1,512]{2,0,1:T(8,128)(2,1)S(1)}, u32[]{:S(2)}, u32[]{:S(2)}) collective-permute-start(bf16[96,1,512]{2,0,1:T(8,128)(2,1)S(1)} %maximum_select_fusion.4), channel_id=1, source_target_pairs={{0,16},{8,24},{16,0},{24,8},{1,17},{9,25},{17,1},{25,9},{2,18},{10... | collective-permute-start | bytes 294920 | tf_op jit(solution)/shard_map/ppermute | solution.py:10
  266.1 4.7 %collective-permute-start.4 = (bf16[192,192]{0,1:T(8,128)(2,1)S(1)}, bf16[192,192]{0,1:T(8,128)(2,1)S(1)}, u32[]{:S(2)}, u32[]{:S(2)}) collective-permute-start(bf16[192,192]{0,1:T(8,128)(2,1)S(1)} %get-tuple-element.10), channel_id=1, source_target_pairs={{0,8},{8,0},{16,24},{24,16},{1,9},{9,1},{17,25},{25,17},{2,10},{10... | collective-permute-start | bytes 221192 | tf_op jit(solution)/shard_map/ppermute | solution.py:10
  270.8 4.7 %collective-permute-start.5 = (bf16[192,192]{0,1:T(8,128)(2,1)S(1)}, bf16[192,192]{0,1:T(8,128)(2,1)S(1)}, u32[]{:S(2)}, u32[]{:S(2)}) collective-permute-start(bf16[192,192]{0,1:T(8,128)(2,1)S(1)} %fusion.12), channel_id=1, source_target_pairs={{0,16},{8,24},{16,0},{24,8},{1,17},{9,25},{17,1},{25,9},{2,18},{10... | collective-permute-start | bytes 221192 | tf_op jit(solution)/shard_map/ppermute | solution.py:10
where the time goes:
time: 308 us; the launch traced here: 307 us
  blocking collectives  143 us (46%)
  other arithmetic  68.6 us (22%)
  matrix products  31.4 us (10%)
  local copies, waits for them, and re-layouts  31.3 us (10%)
  waiting for transfers between devices  17.9 us (6%)
  starting transfers between devices  12.8 us (4%)
    psum x4, blocking collectives, body(): projected = lax.psum(term_full, 'panel').astype(jnp.bfloat16)  143 us
    another operation x16, other arithmetic, body(): jnp.linalg.cholesky(jnp.eye(group_width, dtype=jnp.float32) + gram_total)  48.3 us
    unnamed x7, local copies, waits for them, and re-layouts  27.4 us
    ppermute x6, waiting for transfers between devices, from_partner(): return lax.ppermute(value, axis, pairs)  17.9 us
    another operation x6, other arithmetic, body(): jax.scipy.linalg.solve_triangular(factor, remainder, lower=True)  16.7 us
    dot_general x3, matrix products, body(): lax.dot_general(projected, coupling, (((0,), (0,)), ((), ())), preferred_...  15.5 us
    dot_general x4, matrix products, body(): lax.dot_general(inverse, top_rows, (((1,), (1,)), ((), ())), preferred_el...  13 us
    ppermute x6, starting transfers between devices, from_partner(): return lax.ppermute(value, axis, pairs)  7.62 us
  transfers between devices with their start and end apart: 7, of which 6 were waited for; matrix products, arithmetic and copies ran while one was open for 9% of the time, Pallas kernels for 0%

commit v1 on v0

v1 whole, which is shorter than its diff:
```python
import functools

import jax
import jax.numpy as jnp
from jax import lax
from jax.experimental import pallas as pl
from jax.experimental.pallas import tpu as pltpu
from jax.sharding import PartitionSpec as P

MESH = pl.DeviceIdType.MESH
LEVELS = (3, 2, 1, 0)
SLOT = 16
NT = (((1,), (1,)), ((), ()))
NN = (((1,), (0,)), ((), ()))


def radices(size):
    steps = []
    while size > 1:
        steps.append(min(4, size))
        size //= steps[-1]
    return steps


def mm(a, b, dims):
    return lax.dot_general(a, b, dims, preferred_element_type=jnp.float32)


def mm32(a, b, dims):
    return lax.dot_general(
        a, b, dims, precision=lax.Precision.HIGHEST, preferred_element_type=jnp.float32
    )


def factor_block(block, work):
    n = block.shape[0]
    work[:, :n] = block
    row_pos = lax.broadcasted_iota(jnp.int32, (n, 128), 0)
    lane_pos = lax.broadcasted_iota(jnp.int32, (n, 128), 1)
    rows = lax.broadcasted_iota(jnp.int32, (n, 1), 0)
    m = jnp.where(lane_pos < n, work[...], 0.0) + (lane_pos == row_pos + 64).astype(jnp.float32)
    for j in range(n):
        column = jnp.where(rows > j, m[:, j : j + 1], 0.0)
        m = m - column * (m[j : j + 1, :] * (1.0 / m[j : j + 1, j : j + 1]))
    pivots = jnp.sum(jnp.where(lane_pos == row_pos, m, 0.0), axis=1, keepdims=True)
    m = m * lax.rsqrt(pivots)
    upper = jnp.where(lane_pos >= row_pos, m, 0.0)[:, :n]
    return upper, m[:, 64 : 64 + n]


def eye(n):
    return (
        lax.broadcasted_iota(jnp.int32, (n, n), 0) == lax.broadcasted_iota(jnp.int32, (n, n), 1)
    ).astype(jnp.float32)


def factor_panels(total, width, work):
    count = total.shape[0] // width
    panels = [total[k * width :, k * width : (k + 1) * width] for k in range(count)]
    result = []
    for k in range(count):
        upper, inverse = factor_block(panels[k][:width], work)
        below = None
        if k + 1 < count:
            below = mm32(panels[k][width:], inverse, NT)
            for j in range(k + 1, count):
                at = (j - k - 1) * width
                panels[j] = panels[j] - mm32(below[at:], below[at : at + width], NT)
        result.append((upper, inverse, below))
    return result


def kernel(cube, panel, width, per_slot, leaves, geometry, *refs):
    refs = list(refs)
    take = lambda count: [refs.pop(0) for _ in range(count)]
    labels, columns = take(2)
    inv_hbm = dict(zip(LEVELS, take(4)))
    coup_hbm = dict(zip(LEVELS[:3], take(3)))
    core_out = take(1)[0]
    proj_out = dict(zip(LEVELS, take(4)))
    inv = dict(zip(LEVELS, take(4)))
    coup = dict(zip(LEVELS[:3], take(3)))
    packed, arrived = take(2)
    front = dict(zip(LEVELS, take(4)))
    sent = dict(zip(LEVELS, take(4)))
    got = dict(zip(LEVELS, take(4)))
    full = dict(zip(LEVELS, take(4)))
    gram = dict(zip(LEVELS, take(4)))
    gram_part = dict(zip(LEVELS, take(4)))
    cross = dict(zip(LEVELS[:3], take(3)))
    cross_part = dict(zip(LEVELS[:3], take(3)))
    solved = dict(zip(LEVELS[:3], take(3)))
    work = take(1)[0]
    load_sem, route_send, route_recv, panel_send, panel_recv, cube_send, cube_recv = take(7)

    c = lax.axis_index("cube")
    p = lax.axis_index("panel")

    loads = {}
    for at, level in enumerate(LEVELS):
        loads[level] = [pltpu.make_async_copy(inv_hbm[level], inv[level], load_sem.at[at, 0])]
        if level:
            loads[level].append(
                pltpu.make_async_copy(coup_hbm[level], coup[level], load_sem.at[at, 1])
            )
        for load in loads[level]:
            load.start()

    barrier = pltpu.get_barrier_semaphore()

    def greet(axis, me, size):
        def one(d, carry):
            pl.semaphore_signal(
                barrier, inc=1, device_id={axis: lax.rem(me + d, size)}, device_id_type=MESH
            )
            return carry

        lax.fori_loop(1, size, one, 0)

    greet("cube", c, cube)
    greet("panel", p, panel)

    label = labels[...]
    time_cols = label.shape[1]
    share = cube // leaves
    onehot = lax.broadcasted_iota(jnp.int32, (16, time_cols), 0) == label
    earlier = lax.broadcasted_iota(jnp.int32, (time_cols, time_cols), 0) < (
        lax.broadcasted_iota(jnp.int32, (time_cols, time_cols), 1)
    )
    onehot = onehot.astype(jnp.float32)
    before = mm(onehot.astype(jnp.bfloat16), earlier.astype(jnp.float32).astype(jnp.bfloat16), NN)
    within = jnp.sum(before * onehot, axis=0, keepdims=True).astype(jnp.int32)
    turn = jnp.zeros_like(within)
    for step in range(1, share):
        turn = turn + (within >= step * per_slot).astype(jnp.int32)
    target = (label * share + turn) * SLOT + within - turn * per_slot
    dispatch = (
        (lax.broadcasted_iota(jnp.int32, (cube * SLOT, time_cols), 0) == target)
        .astype(jnp.float32)
        .astype(jnp.bfloat16)
    )
    for j in range(4):
        block = mm(dispatch, columns[j], NN).astype(jnp.bfloat16)
        packed[:, j] = block.reshape(cube, SLOT, block.shape[1])

    pl.semaphore_wait(barrier, cube + panel - 2)

    def route(d):
        to = lax.rem(c + d, cube)
        return pltpu.make_async_remote_copy(
            src_ref=packed.at[to],
            dst_ref=arrived.at[c],
            send_sem=route_send.at[d],
            recv_sem=route_recv.at[d],
            device_id={"cube": to},
            device_id_type=MESH,
        )

    def each(low, high, do):
        def one(d, carry):
            do(d)
            return carry

        lax.fori_loop(low, high, one, 0)

    each(1, cube, lambda d: route(d).start())
    arrived[c] = packed[c]
    each(1, cube, lambda d: route(d).wait_recv())
    out_pos = lax.broadcasted_iota(jnp.int32, (width, cube * SLOT), 0)
    in_pos = lax.broadcasted_iota(jnp.int32, (width, cube * SLOT), 1)
    select = jnp.zeros((width, cube * SLOT), jnp.float32)
    for s in range(cube):
        hit = (in_pos - s * SLOT == out_pos - s * per_slot) & (out_pos >= s * per_slot)
        hit = hit & (out_pos < (s + 1) * per_slot)
        select = select + hit.astype(jnp.float32)
    select = select.astype(jnp.bfloat16)
    first_size, _ = geometry[3][:2]
    first_rank = lax.rem(c, first_size)
    for j in range(4):
        mine = mm(select, arrived[:, j].reshape(cube * SLOT, arrived.shape[3]), NN)
        front[3][first_rank, j] = mine.astype(jnp.bfloat16)

    pending = []

    def settle(copy, radix):
        each(1, radix, lambda d: copy(d).wait_recv())

    def fold(slots, stage, radix):
        value = slots[stage, 0].astype(jnp.float32)
        for s in range(1, radix):
            value = value + slots[stage, s].astype(jnp.float32)
        return value

    def group_copy(level, phase, src, dst, size, d):
        rank = lax.rem(c, size)
        to = c - rank + lax.rem(rank + d, size)
        return pltpu.make_async_remote_copy(
            src_ref=src,
            dst_ref=dst,
            send_sem=cube_send.at[level, phase, d],
            recv_sem=cube_recv.at[level, phase, d],
            device_id={"cube": to},
            device_id_type=MESH,
        )

    def share_front(level, size, source):
        rank = lax.rem(c, size)
        if source is not None:
            front[level][rank] = source
        if size > 1:
            copy = lambda d: group_copy(
                level, 0, front[level].at[rank], front[level].at[rank], size, d
            )
            each(1, size, lambda d: copy(d).start())
            each(1, size, lambda d: copy(d).wait_recv())
            pending.append((1, size, copy))

    share_front(3, first_size, None)

    for at, level in enumerate(LEVELS):
        size, rows, part = geometry[level]
        wide = size * width
        rank = lax.rem(c, size)
        stripe = front[level].shape[3]
        top = front[level][:, 0].reshape(wide, stripe)
        loads[level][0].wait()

        def term(q, level=level, part=part, top=top):
            return mm(top, inv[level][pl.ds(pl.multiple_of(q * part, part), part), :], NT)

        def scatter(d, level=level):
            to = lax.rem(p + d, panel)
            return pltpu.make_async_remote_copy(
                src_ref=sent[level].at[d],
                dst_ref=got[level].at[d],
                send_sem=panel_send.at[level, 0, d],
                recv_sem=panel_recv.at[level, 0, d],
                device_id={"panel": to},
                device_id_type=MESH,
            )

        def send_term(d, level=level, term=term, scatter=scatter):
            sent[level][d] = term(lax.rem(p + d, panel)).astype(jnp.bfloat16)
            scatter(d).start()

        each(1, panel, send_term)
        own = term(p)
        for d in range(1, panel):
            scatter(d).wait_recv()
            own = own + got[level][d].astype(jnp.float32)
        own = own.astype(jnp.bfloat16)
        proj_out[level][...] = own
        full[level][p] = own

        def gather(d, level=level):
            to = lax.rem(p + d, panel)
            return pltpu.make_async_remote_copy(
                src_ref=full[level].at[p],
                dst_ref=full[level].at[p],
                send_sem=panel_send.at[level, 1, d],
                recv_sem=panel_recv.at[level, 1, d],
                device_id={"panel": to},
                device_id_type=MESH,
            )

        each(1, panel, lambda d, gather=gather: gather(d).start())
        pending.append((1, panel, scatter))
        pending.append((1, panel, gather))

        if level:
            loads[level][1].wait()

        def add_chunk(q, first, level=level, part=part):
            chunk = full[level][q]
            value = mm(chunk, chunk, NT)
            gram[level][...] = value if first else gram[level][...] + value
            for j in range(level):
                block = coup[level][j, pl.ds(pl.multiple_of(q * part, part), part), :]
                value = mm(chunk, block, NN)
                cross[level][j] = value if first else cross[level][j] + value

        add_chunk(p, True)

        def receive(d, gather=gather, add_chunk=add_chunk):
            gather(d).wait_recv()
            add_chunk(lax.rem(p + panel - d, panel), False)

        each(1, panel, receive)

        steps = radices(size)
        stride = 1
        copies = None
        for stage, radix in enumerate(steps):
            if stage and level:
                settle(copies[1], radix_before)
                cross[level][...] = fold(cross_part[level], stage - 1, radix_before)
            digit = lax.rem(lax.div(rank, stride), radix)
            copies = []
            for kind, slots, acc in ((0, gram_part, gram), (1, cross_part, cross)):
                if kind and not level:
                    continue
                slots[level][stage, digit] = acc[level][...].astype(slots[level].dtype)

                def copy(d, kind=kind, slot=slots[level], stage=stage, digit=digit, stride=stride, radix=radix, level=level):
                    return pltpu.make_async_remote_copy(
                        src_ref=slot.at[stage, digit],
                        dst_ref=slot.at[stage, digit],
                        send_sem=cube_send.at[level, 1 + 2 * stage + kind, d],
                        recv_sem=cube_recv.at[level, 1 + 2 * stage + kind, d],
                        device_id={"cube": c + (lax.rem(digit + d, radix) - digit) * stride},
                        device_id_type=MESH,
                    )

                each(1, radix, lambda d, copy=copy: copy(d).start())
                pending.append((1, radix, copy))
                copies.append(copy)
            settle(copies[0], radix)
            gram[level][...] = fold(gram_part[level], stage, radix)
            radix_before, stride = radix, stride * radix
        total = eye(wide) + gram[level][...]
        blocks = factor_panels(total, width, work)
        if not level:
            for k, (upper, _, below) in enumerate(blocks):
                low = k * width
                if k:
                    core_out[:low, low : low + width] = jnp.zeros((low, width), jnp.float32)
                core_out[low : low + width, low : low + width] = mm32(eye(width), upper, NT)
                if below is not None:
                    core_out[low + width :, low : low + width] = below
            break
        if steps:
            settle(copies[1], radix_before)
            summed_all = fold(cross_part[level], len(steps) - 1, radix_before)
        for j in range(level):
            summed = summed_all[j] if steps else cross[level][j]
            for k, (_, inverse, below) in enumerate(blocks):
                low = k * width
                right = front[level][k, j + 1].astype(jnp.float32) - summed[low : low + width]
                for earlier_k in range(k):
                    at_row = (k - earlier_k - 1) * width
                    right = right - mm32(
                        blocks[earlier_k][2][at_row : at_row + width], values[earlier_k], NN
                    )
                values = [] if k == 0 else values
                values.append(mm32(inverse, right, NN))
                solved[level][k, j] = values[k].astype(jnp.bfloat16)
        share_front(level - 1, geometry[level - 1][0], solved[level][rank])

    each(1, cube, lambda d: route(d).wait_send())
    for low, high, copy in pending:
        each(low, high, lambda d, copy=copy: copy(d).wait_send())


def body(
    cube,
    panel,
    columns,
    leaf_of,
    inverse_root,
    inverse_upper,
    inverse_middle,
    inverse_leaf,
    coupling_upper,
    coupling_middle,
    coupling_leaf,
):
    time_cols, _, stripe = columns.shape
    leaves = min(8, cube)
    leaf_share = cube // leaves
    per_slot = max(1, (2 * time_cols // leaves + leaf_share - 1) // leaf_share)
    width = cube * per_slot
    inverses = [inverse_leaf, inverse_middle, inverse_upper, inverse_root]
    couplings = [
        jnp.transpose(x, (1, 0, 2)) for x in (coupling_leaf, coupling_middle, coupling_upper)
    ]
    geometry = {}
    for level, inverse in zip(LEVELS, inverses):
        rows = inverse.shape[0]
        geometry[level] = (cube // min(2**level, cube), rows, rows // panel)
    wide = {level: geometry[level][0] * width for level in LEVELS}
    part = {level: geometry[level][2] for level in LEVELS}
    size = {level: geometry[level][0] for level in LEVELS}
    vm = pltpu.VMEM
    scratch = [vm(x.shape, x.dtype) for x in inverses]
    scratch += [vm(x.shape, x.dtype) for x in couplings]
    scratch += [vm((cube, 4, SLOT, stripe), jnp.bfloat16)] * 2
    scratch += [vm((size[l], l + 1, width, stripe), jnp.bfloat16) for l in LEVELS]
    for _ in range(3):
        scratch += [vm((panel, wide[l], part[l]), jnp.bfloat16) for l in LEVELS]
    scratch += [vm((wide[l], wide[l]), jnp.float32) for l in LEVELS]
    for l in LEVELS:
        steps = radices(size[l]) or [1]
        kind = jnp.float32 if size[l] <= 4 else jnp.bfloat16
        scratch += [vm((len(steps), max(steps), wide[l], wide[l]) if size[l] > 1 else (1, 1, 8, 128), kind)]
    scratch += [vm((l, wide[l], stripe), jnp.float32) for l in LEVELS[:3]]
    for l in LEVELS[:3]:
        steps = radices(size[l]) or [1]
        scratch += [vm((len(steps), max(steps), l, wide[l], stripe), jnp.bfloat16)]
    scratch += [vm((size[l], l, width, stripe), jnp.bfloat16) for l in LEVELS[:3]]
    scratch += [vm((width, 128), jnp.float32)]
    dma = pltpu.SemaphoreType.DMA
    scratch += [dma((4, 2)), dma((cube,)), dma((cube,)), dma((4, 2, panel)), dma((4, 2, panel))]
    scratch += [dma((4, 5, cube)), dma((4, 5, cube))]
    outs = [jax.ShapeDtypeStruct((wide[0], wide[0]), jnp.float32)]
    outs += [jax.ShapeDtypeStruct((wide[l], part[l]), jnp.bfloat16) for l in LEVELS]
    in_vmem = pl.BlockSpec(memory_space=pltpu.VMEM)
    in_any = pl.BlockSpec(memory_space=pl.ANY)
    core, leaf, middle, upper, root = pl.pallas_call(
        functools.partial(kernel, cube, panel, width, per_slot, leaves, geometry),
        out_shape=outs,
        in_specs=[in_vmem, in_vmem] + [in_any] * 7,
        out_specs=[in_vmem] * 5,
        scratch_shapes=scratch,
        compiler_params=pltpu.CompilerParams(
            collective_id=0, has_side_effects=True, vmem_limit_bytes=58 * 2**20
        ),
    )(
        jnp.transpose(leaf_of),
        jnp.transpose(columns, (1, 0, 2)),
        *inverses,
        *couplings,
    )
    return (core, root.T, upper.T, middle.T, leaf.T)


def solution(mesh):
    in_specs = (
        P("cube", None, "panel"),
        P("cube", None),
        P("cube", "panel"),
        P("cube", "panel"),
        P("cube", "panel"),
        P("cube", "panel"),
        P("cube", None, "panel"),
        P("cube", None, "panel"),
        P("cube", None, "panel"),
    )
    out_specs = (
        P(),
        P(("cube", "panel"), None),
        P(("cube", "panel"), None),
        P(("cube", "panel"), None),
        P(("cube", "panel"), None),
    )
    run = functools.partial(body, mesh.shape["cube"], mesh.shape["panel"])
    return jax.shard_map(run, mesh=mesh, in_specs=in_specs, out_specs=out_specs, check_vma=False)
```

time: 308 us -> 171 us (0.56)
  Pallas kernels: 0 us -> 151 us
  blocking collectives: 143 us -> 0 us
  other arithmetic: 68.6 us -> 0 us
  matrix products: 31.4 us -> 0 us
  waiting for transfers between devices: 17.9 us -> 0 us
  local copies, waits for them, and re-layouts: 31.3 us -> 16.8 us
  starting transfers between devices: 12.8 us -> 0 us
    pallas_call x0 -> x1, Pallas kernels: none -> 151 us  [body(): pl.pallas_call(functools.partial(kernel, cube, panel, width, per_slot, le...]
    psum x4 -> x0, blocking collectives: 143 us -> none  [body(): projected = lax.psum(term_full, 'panel').astype(jnp.bfloat16)]
    another operation x23 -> x0, other arithmetic: 65 us -> none  [the longest x16 48.3 us: body(): jnp.linalg.cholesky(jnp.eye(group_width, dtype=jnp.float32) + gram_total)]
    dot_general x12 -> x0, matrix products: 29.8 us -> none  [the longest x3 15.5 us: body(): lax.dot_general(projected, coupling, (((0,), (0,)), ((), ())), preferred_...]
    ppermute x6 -> x0, waiting for transfers between devices: 17.9 us -> none  [from_partner(): return lax.ppermute(value, axis, pairs)]
    unnamed x7, local copies, waits for them, and re-layouts: 27.4 us -> 16.8 us
    ppermute x6 -> x0, starting transfers between devices: 7.62 us -> none  [from_partner(): return lax.ppermute(value, axis, pairs)]
    all_to_all x1 -> x0, starting transfers between devices: 5.16 us -> none  [body(): lax.all_to_all(packed, 'cube', split_axis=0, concat_axis=0, tiled=True)]
  transfers between devices with their start and end apart: 7 -> 0, of which waited for: 6 -> 0; matrix products, arithmetic and copies ran while one was open for 9% -> 0% of each run, Pallas kernels for 0% -> 0%
where the time goes in v1:
time: 171 us; the launch traced here: 168 us
  Pallas kernels  151 us (88%)
  local copies, waits for them, and re-layouts  16.8 us (10%)
    pallas_call x1, Pallas kernels, body(): pl.pallas_call(functools.partial(kernel, cube, panel, width, per_slot, le...  151 us
    unnamed x7, local copies, waits for them, and re-layouts  16.8 us

profile of v1, /device:TPU:0, one launch (start us, length us, event | category | flops | bytes accessed | tf_op | source)
XLA Modules:
  0.0 168.5 jit_solution(18103210110227998154)
XLA Ops:
  0.6 1.6 copy.19
  2.2 7.9 %copy.18 = bf16[4096,2,512]{2,0,1:T(8,128)(2,1)} copy(bf16[4096,2,512]{2,1,0:T(2,128)(2,1)} %param.16) | data formatting | bytes 16777216 | tf_op args[7]
  10.1 151.0 %shard_map.128 = (f32[192,192]{1,0:T(8,128)}, bf16[48,512]{1,0:T(8,128)(2,1)}, bf16[48,512]{1,0:T(8,128)(2,1)}, bf16[96,256]{1,0:T(8,128)(2,1)}, bf16[192,128]{1,0:T(8,128)(2,1)}) custom-call(s32[1,24]{1,0:T(1,128)} %bitcast.21, bf16[4,24,512]{2,1,0:T(8,128)(2,1)} %bitcast.16, bf16[4096,512]{1,0:T(8,128)(2,1)} %refs_2_.1, bf16[4096,512]{1,0:T(8,128)(2,1)} %refs_3_.1, ...), custom_call_target="tpu_custom_call" | custom-call | tf_op jit(solution)/shard_map/pallas_call | solution.py:408
  161.2 1.6 copy.25
  162.8 1.4 copy.26
  164.2 1.4 copy.27
  165.6 1.4 copy.28
  167.1 1.4 copy.29

commit v2 on v1

--- a/solution.py
+++ b/solution.py
@@ -37,11 +37,25 @@
     work[:, :n] = block
     row_pos = lax.broadcasted_iota(jnp.int32, (n, 128), 0)
     lane_pos = lax.broadcasted_iota(jnp.int32, (n, 128), 1)
-    rows = lax.broadcasted_iota(jnp.int32, (n, 1), 0)
     m = jnp.where(lane_pos < n, work[...], 0.0) + (lane_pos == row_pos + 64).astype(jnp.float32)
-    for j in range(n):
-        column = jnp.where(rows > j, m[:, j : j + 1], 0.0)
-        m = m - column * (m[j : j + 1, :] * (1.0 / m[j : j + 1, j : j + 1]))
+    done = []
+    for j in range(0, n, 2):
+        if j and j % 8 == 0:
+            done.append(m[:8])
+            m = m[8:]
+        at = j % 8
+        shape = m.shape
+        here = row_pos[: shape[0]]
+        first = jnp.broadcast_to(m[:, j : j + 1], shape)
+        second = jnp.broadcast_to(m[:, j + 1 : j + 2], shape)
+        a, b, d = first[at : at + 1], first[at + 1 : at + 2], second[at + 1 : at + 2]
+        over_a, over_d = 1.0 / a, a * (1.0 / (a * d - b * b))
+        ratio = b * over_a
+        top, next_row = m[at : at + 1], m[at + 1 : at + 2]
+        low = jnp.where(here > at + 1, second - ratio * first, 0.0)
+        first = jnp.where(here > at, first, 0.0)
+        m = m - first * (top * over_a) - low * ((next_row - ratio * top) * over_d)
+    m = jnp.concatenate(done + [m], axis=0)
     pivots = jnp.sum(jnp.where(lane_pos == row_pos, m, 0.0), axis=1, keepdims=True)
     m = m * lax.rsqrt(pivots)
     upper = jnp.where(lane_pos >= row_pos, m, 0.0)[:, :n]
@@ -82,6 +96,8 @@
     coup = dict(zip(LEVELS[:3], take(3)))
     packed, arrived = take(2)
     front = dict(zip(LEVELS, take(4)))
+    twin_sent = dict(zip(LEVELS, take(4)))
+    twin_got = dict(zip(LEVELS, take(4)))
     sent = dict(zip(LEVELS, take(4)))
     got = dict(zip(LEVELS, take(4)))
     full = dict(zip(LEVELS, take(4)))
@@ -95,6 +111,8 @@
 
     c = lax.axis_index("cube")
     p = lax.axis_index("panel")
+    chips = panel // 2
+    chip, core = lax.div(p, 2), lax.rem(p, 2)
 
     loads = {}
     for at, level in enumerate(LEVELS):
@@ -225,67 +243,90 @@
         top = front[level][:, 0].reshape(wide, stripe)
         loads[level][0].wait()
 
-        def term(q, level=level, part=part, top=top):
-            return mm(top, inv[level][pl.ds(pl.multiple_of(q * part, part), part), :], NT)
-
-        def scatter(d, level=level):
-            to = lax.rem(p + d, panel)
+        def term(z, core, level=level, part=part, top=top):
+            at_row = pl.multiple_of((2 * z + core) * part, part)
+            return mm(top, inv[level][pl.ds(at_row, part), :], NT)
+
+        def panel_copy(kind, src, dst, d, z, core, level=level):
             return pltpu.make_async_remote_copy(
-                src_ref=sent[level].at[d],
-                dst_ref=got[level].at[d],
-                send_sem=panel_send.at[level, 0, d],
-                recv_sem=panel_recv.at[level, 0, d],
-                device_id={"panel": to},
+                src_ref=src,
+                dst_ref=dst,
+                send_sem=panel_send.at[level, kind, d],
+                recv_sem=panel_recv.at[level, kind, d],
+                device_id={"panel": 2 * z + core},
                 device_id_type=MESH,
             )
 
-        def send_term(d, level=level, term=term, scatter=scatter):
-            sent[level][d] = term(lax.rem(p + d, panel)).astype(jnp.bfloat16)
+        def to_twin(d, level=level, panel_copy=panel_copy):
+            return panel_copy(0, twin_sent[level].at[d], twin_got[level].at[d], d, chip, 1 - core)
+
+        def scatter(d, level=level, panel_copy=panel_copy):
+            to = lax.rem(chip + d, chips)
+            return panel_copy(1, sent[level].at[d], got[level].at[d], d, to, core)
+
+        def send_twin(d, level=level, term=term, to_twin=to_twin):
+            twin_sent[level][d] = term(lax.rem(chip + d, chips), 1 - core).astype(jnp.bfloat16)
+            to_twin(d).start()
+
+        def send_term(d, level=level, term=term, to_twin=to_twin, scatter=scatter):
+            mine = term(lax.rem(chip + d, chips), core)
+            to_twin(d).wait_recv()
+            sent[level][d] = (mine + twin_got[level][d].astype(jnp.float32)).astype(jnp.bfloat16)
             scatter(d).start()
 
-        each(1, panel, send_term)
-        own = term(p)
-        for d in range(1, panel):
+        each(1, chips, send_twin)
+        send_twin(0)
+        each(1, chips, send_term)
+        own = term(chip, core)
+        to_twin(0).wait_recv()
+        own = own + twin_got[level][0].astype(jnp.float32)
+        for d in range(1, chips):
             scatter(d).wait_recv()
             own = own + got[level][d].astype(jnp.float32)
         own = own.astype(jnp.bfloat16)
+        full[level][chip, core] = own
+
+        def gather(d, level=level, panel_copy=panel_copy):
+            here = full[level].at[chip, core]
+            return panel_copy(2, here, here, d, lax.rem(chip + d, chips), core)
+
+        def forward(d, level=level, panel_copy=panel_copy):
+            here = full[level].at[lax.rem(chip + chips - d, chips), core]
+            return panel_copy(3, here, here, d, chip, 1 - core)
+
+        each(1, chips, lambda d, gather=gather: gather(d).start())
+        forward(0).start()
         proj_out[level][...] = own
-        full[level][p] = own
-
-        def gather(d, level=level):
-            to = lax.rem(p + d, panel)
-            return pltpu.make_async_remote_copy(
-                src_ref=full[level].at[p],
-                dst_ref=full[level].at[p],
-                send_sem=panel_send.at[level, 1, d],
-                recv_sem=panel_recv.at[level, 1, d],
-                device_id={"panel": to},
-                device_id_type=MESH,
-            )
-
-        each(1, panel, lambda d, gather=gather: gather(d).start())
-        pending.append((1, panel, scatter))
-        pending.append((1, panel, gather))
+        pending.append((0, chips, to_twin))
+        pending.append((1, chips, scatter))
+        pending.append((1, chips, gather))
+        pending.append((0, chips, forward))
 
         if level:
             loads[level][1].wait()
 
-        def add_chunk(q, first, level=level, part=part):
-            chunk = full[level][q]
+        def add_chunk(z, core, first, level=level, part=part):
+            chunk = full[level][z, core]
             value = mm(chunk, chunk, NT)
             gram[level][...] = value if first else gram[level][...] + value
             for j in range(level):
-                block = coup[level][j, pl.ds(pl.multiple_of(q * part, part), part), :]
-                value = mm(chunk, block, NN)
+                at_row = pl.multiple_of((2 * z + core) * part, part)
+                value = mm(chunk, coup[level][j, pl.ds(at_row, part), :], NN)
                 cross[level][j] = value if first else cross[level][j] + value
 
-        add_chunk(p, True)
-
-        def receive(d, gather=gather, add_chunk=add_chunk):
+        add_chunk(chip, core, True)
+
+        def receive(d, gather=gather, forward=forward, add_chunk=add_chunk):
             gather(d).wait_recv()
-            add_chunk(lax.rem(p + panel - d, panel), False)
-
-        each(1, panel, receive)
+            forward(d).start()
+            add_chunk(lax.rem(chip + chips - d, chips), core, False)
+
+        def receive_twin(d, forward=forward, add_chunk=add_chunk):
+            forward(d).wait_recv()
+            add_chunk(lax.rem(chip + chips - d, chips), 1 - core, False)
+
+        each(1, chips, receive)
+        each(0, chips, receive_twin)
 
         steps = radices(size)
         stride = 1
@@ -351,6 +392,11 @@
         each(low, high, lambda d, copy=copy: copy(d).wait_send())
 
 
+def hand_out(*refs):
+    for source, result in zip(refs[:5], refs[5:]):
+        result[...] = source[...]
+
+
 def body(
     cube,
     panel,
@@ -385,8 +431,9 @@
     scratch += [vm(x.shape, x.dtype) for x in couplings]
     scratch += [vm((cube, 4, SLOT, stripe), jnp.bfloat16)] * 2
     scratch += [vm((size[l], l + 1, width, stripe), jnp.bfloat16) for l in LEVELS]
-    for _ in range(3):
-        scratch += [vm((panel, wide[l], part[l]), jnp.bfloat16) for l in LEVELS]
+    for _ in range(4):
+        scratch += [vm((panel // 2, wide[l], part[l]), jnp.bfloat16) for l in LEVELS]
+    scratch += [vm((panel // 2, 2, wide[l], part[l]), jnp.bfloat16) for l in LEVELS]
     scratch += [vm((wide[l], wide[l]), jnp.float32) for l in LEVELS]
     for l in LEVELS:
         steps = radices(size[l]) or [1]
@@ -399,7 +446,7 @@
     scratch += [vm((size[l], l, width, stripe), jnp.bfloat16) for l in LEVELS[:3]]
     scratch += [vm((width, 128), jnp.float32)]
     dma = pltpu.SemaphoreType.DMA
-    scratch += [dma((4, 2)), dma((cube,)), dma((cube,)), dma((4, 2, panel)), dma((4, 2, panel))]
+    scratch += [dma((4, 2)), dma((cube,)), dma((cube,)), dma((4, 4, panel // 2)), dma((4, 4, panel // 2))]
     scratch += [dma((4, 5, cube)), dma((4, 5, cube))]
     outs = [jax.ShapeDtypeStruct((wide[0], wide[0]), jnp.float32)]
     outs += [jax.ShapeDtypeStruct((wide[l], part[l]), jnp.bfloat16) for l in LEVELS]
@@ -420,6 +467,12 @@
         *inverses,
         *couplings,
     )
+    core, leaf, middle, upper, root = pl.pallas_call(
+        hand_out,
+        out_shape=outs,
+        in_specs=[in_vmem] * 5,
+        out_specs=[in_vmem] * 5,
+    )(core, leaf, middle, upper, root)
     return (core, root.T, upper.T, middle.T, leaf.T)
 
 

time: 171 us -> 133 us (0.78); the launches traced: 168 us -> 132 us
  Pallas kernels: 151 us -> 122 us
  local copies, waits for them, and re-layouts: 16.8 us -> 9.49 us
    pallas_call x1, Pallas kernels: 151 us -> 121 us  [body(): pl.pallas_call(functools.partial(kernel, cube, panel, width, per_slot, le...]
    unnamed x7 -> x2, local copies, waits for them, and re-layouts: 16.8 us -> 9.49 us
    pallas_call x0 -> x1, Pallas kernels: none -> 1.73 us  [body(): pl.pallas_call(hand_out, out_shape=outs, in_specs=[in_vmem] * 5, out_spec...]
where the time goes in v2:
time: 133 us; the launch traced here: 132 us
  Pallas kernels  122 us (92%)
  local copies, waits for them, and re-layouts  9.49 us (7%)
    pallas_call x1, Pallas kernels, body(): pl.pallas_call(functools.partial(kernel, cube, panel, width, per_slot, le...  121 us
    unnamed x2, local copies, waits for them, and re-layouts  9.49 us

profile of v2, /device:TPU:0, one launch (start us, length us, event | category | flops | bytes accessed | tf_op | source)
XLA Modules:
  0.0 132.4 jit_solution(10893665760754073778)
XLA Ops:
  0.6 1.6 %copy.19 = bf16[24,4,512]{2,0,1:T(8,128)(2,1)} copy(bf16[24,4,512]{2,1,0:T(4,128)(2,1)} %param.9) | data formatting | bytes 196608 | tf_op args[0]
  2.2 7.9 %copy.18 = bf16[4096,2,512]{2,0,1:T(8,128)(2,1)} copy(bf16[4096,2,512]{2,1,0:T(2,128)(2,1)} %param.16) | data formatting | bytes 16777216 | tf_op args[7]
  10.1 120.6 %shard_map.128 = (f32[192,192]{1,0:T(8,128)}, bf16[48,512]{1,0:T(8,128)(2,1)}, bf16[48,512]{1,0:T(8,128)(2,1)}, bf16[96,256]{1,0:T(8,128)(2,1)}, bf16[192,128]{1,0:T(8,128)(2,1)}) custom-call(s32[1,24]{1,0:T(1,128)} %bitcast.17, bf16[4,24,512]{2,1,0:T(8,128)(2,1)} %bitcast.16, bf16[4096,512]{1,0:T(8,128)(2,1)} %refs_2_.1, bf16[4096,512]{1,0:T(8,128)(2,1)} %refs_3_.1, ...), custom_call_target="tpu_custom_call" | custom-call | tf_op jit(solution)/shard_map/pallas_call | solution.py:455
  130.7 1.7 %shard_map.129 = (f32[192,192]{1,0:T(8,128)}, bf16[48,512]{1,0:T(8,128)(2,1)}, bf16[48,512]{1,0:T(8,128)(2,1)}, bf16[96,256]{1,0:T(8,128)(2,1)}, bf16[192,128]{1,0:T(8,128)(2,1)}) custom-call(f32[192,192]{1,0:T(8,128)} %get-tuple-element.15.refs_0_, bf16[48,512]{1,0:T(8,128)(2,1)} %get-tuple-element.16.refs_1_, bf16[48,512]{1,0:T(8,128)(2,1)} %get-tuple-element.17.refs_2_, ...), custom_call_target="tpu_custom_call" | custom-call | tf_op jit(solution)/shard_map/pallas_call | solution.py:470
